TPU v7x, 32 devices: a whole 2x2x4 slice. The times are simulated.
32 devices in a mesh: dp: 8 (over y, x, core), shard: 4 (over z).
Axes of the slice: x: 2, y: 2, z: 4, core: 2. Of those that a mesh axis runs over, the one named last changes fastest.
Arguments:
- momentum: float32 [4096, 7168], P('dp', 'shard'), may hold values from -6 to 6
- gradient: bfloat16 [4096, 7168], P('dp', 'shard'), may hold values from -120 to 120
Outputs:
- new_momentum: float32 [4096, 7168], P('dp', 'shard')
- update: float32 [4096, 7168], P('dp', 'shard')
All inputs are finite; a program needn't handle non-finite values.
Results may differ from a plain program's by a relative error of at most 0.0038.
The roundings to bfloat16 on the way count: a program that leaves them out, or rounds other values in their place, can miss the bound.
Values may be sent and summed in bfloat16 or wider, within the bound.
No kernel may reach another device: no remote copies, remote signals or barrier semaphores. Data moves between devices by JAX's collectives and lax.ppermute only.
A program may use at most 64 MiB of HBM per device.

v0:
```python
import math
import jax
import jax.numpy as jnp
from jax import lax
from jax.sharding import PartitionSpec as P

D = 7168
STEPS = 2
momentum_decay = 0.95
linear_term = 3.4445
cubic_term = -4.775
quintic_term = 2.0315


def apply_panel(gram_panel, right_side):
    return jnp.dot(gram_panel, right_side, preferred_element_type=jnp.float32)


def body(momentum, gradient):
    grad_full = gradient.astype(jnp.float32)
    new_momentum = momentum_decay * momentum + grad_full
    current = grad_full + momentum_decay * new_momentum
    for iteration in range(STEPS):
        matrix = current.astype(jnp.bfloat16)
        column_panel = lax.all_gather(matrix, "dp", axis=0, tiled=True)
        summed_part = lax.psum_scatter(
            lax.dot_general(
                matrix, column_panel, (((1,), (1,)), ((), ())), preferred_element_type=jnp.float32
            ),
            "shard",
            scatter_dimension=0,
            tiled=True,
        )
        gram_part = summed_part.astype(jnp.bfloat16)
        gram_panel = lax.all_gather(gram_part, "shard", axis=0, tiled=True)
        square_sum = lax.psum(jnp.sum(jnp.square(gram_part.astype(jnp.float32))), ("dp", "shard"))
        inverse_norm = lax.rsqrt(square_sum)
        root_scale = jnp.sqrt(inverse_norm)
        matrix_full = matrix.astype(jnp.float32)
        first_product = apply_panel(gram_panel, column_panel)
        mixture = (
            cubic_term * root_scale * matrix_full
            + quintic_term * root_scale * inverse_norm * first_product
        ).astype(jnp.bfloat16)
        second_product = apply_panel(gram_panel, lax.all_gather(mixture, "dp", axis=0, tiled=True))
        current = linear_term * root_scale * matrix_full + inverse_norm * second_product
    update = math.sqrt(D) * current
    return (new_momentum, update)


def solution(mesh):
    in_specs = (P("dp", "shard"), P("dp", "shard"))
    out_specs = (P("dp", "shard"), P("dp", "shard"))
    return jax.shard_map(body, mesh=mesh, in_specs=in_specs, out_specs=out_specs, check_vma=False)
```

profile of v0, /device:TPU:0, one launch (start us, length us, event | category | flops | bytes accessed | tf_op | source)
XLA Modules:
  0.0 889.7 jit_solution(13144774973173821033)
XLA Ops:
  7.2 0.0 all-gather.7.cloned.1.call-start
  7.2 5.7 fusion
  12.9 0.0 all-gather.7.cloned.1.call-update
  12.9 0.0 reduce-scatter.3.cloned.1.call-start
  13.0 83.7 %all-gather.7.cloned.1.call-done = bf16[4096,1792]{1,0:T(8,128)(2,1)} async-done(((bf16[512,1792]{1,0:T(8,128)(2,1)}), bf16[4096,1792]{1,0:T(8,128)(2,1)}) %all-gather.7.cloned.1.call-update) | async-done | bytes 14680080 | tf_op jit(solution)/shard_map/all_gather | solution.py:25
  96.7 13.5 %fusion.9 = f32[512,4096]{1,0:T(8,128)} fusion(bf16[512,1792]{1,0:T(8,128)(2,1)} %get-tuple-element.6, bf16[4096,1792]{1,0:T(8,128)(2,1)} %all-gather.7.cloned.1.call-done), kind=kOutput, calls=%fused_computation.17 | convolution fusion | flops 7516192768 | bytes 24903680 | tf_op jit(solution)/shard_map/dot_general | solution.py:27
  110.2 0.0 reduce-scatter.3.cloned.1.call-update
  110.2 0.0 copy-start
  110.2 0.0 all-gather.9.cloned.1.call-start
  110.3 144.7 %reduce-scatter.3.cloned.1.call-done = f32[128,4096]{1,0:T(8,128)} async-done(((f32[512,4096]{1,0:T(8,128)}), f32[128,4096]{1,0:T(8,128)}) %reduce-scatter.3.cloned.1.call-update) | async-done | bytes 2097168 | tf_op jit(solution)/shard_map/reduce_scatter | solution.py:26
  255.0 3.7 multiply_reduce_fusion.1
  258.7 0.0 all-gather.9.cloned.1.call-update
  258.7 0.0 all-gather.11.cloned.1.call-start
  258.7 46.6 %psum.14 = f32[]{:T(128)} all-reduce(f32[]{:T(128)} %get-tuple-element.4), channel_id=1, replica_groups=mesh['dp'=8,'shard'=4] {'dp','shard'}, use_global_device_ids=true, to_apply=%region_2.0 | all-reduce | flops 1 | bytes 8 | tf_op jit(solution)/shard_map/psum | solution.py:36
  306.1 35.1 %all-gather.9.cloned.1.call-done = bf16[512,4096]{1,0:T(8,128)(2,1)} async-done(((bf16[128,4096]{1,0:T(8,128)(2,1)}), bf16[512,4096]{1,0:T(8,128)(2,1)}) %all-gather.9.cloned.1.call-update) | async-done | bytes 4194320 | tf_op jit(solution)/shard_map/all_gather | solution.py:35
  341.2 0.0 copy-done
  341.2 14.2 %fusion.4 = bf16[512,1792]{1,0:T(8,128)(2,1)} fusion(bf16[512,1792]{1,0:T(8,128)(2,1)S(1)} %copy-done, bf16[512,4096]{1,0:T(8,128)(2,1)} %all-gather.9.cloned.1.call-done, bf16[4096,1792]{1,0:T(8,128)(2,1)} %all-gather.7.cloned.1.call-done, f32[]{:T(128)S(6)} %mul.94, f32[]{:T(128)S(6)} %mul.90), kind=kOutput, calls=%fused_computation.10 | convolution fusion | flops 7520780288 | bytes 22544392 | tf_op jit(solution)/shard_map/dot_general | solution.py:16
  355.4 0.0 all-gather.11.cloned.1.call-update
  355.4 0.0 all-gather.13.cloned.1.call-start
  355.4 79.4 %all-gather.11.cloned.1.call-done = bf16[4096,1792]{1,0:T(8,128)(2,1)} async-done(((bf16[512,1792]{1,0:T(8,128)(2,1)}), bf16[4096,1792]{1,0:T(8,128)(2,1)}) %all-gather.11.cloned.1.call-update) | async-done | bytes 14680080 | tf_op jit(solution)/shard_map/all_gather | solution.py:45
  434.9 14.2 %fusion.2 = bf16[512,1792]{1,0:T(8,128)(2,1)} fusion(bf16[512,1792]{1,0:T(8,128)(2,1)S(1)} %copy-done, bf16[512,4096]{1,0:T(8,128)(2,1)} %all-gather.9.cloned.1.call-done, bf16[4096,1792]{1,0:T(8,128)(2,1)} %all-gather.11.cloned.1.call-done, f32[]{:T(128)S(6)} %rsqrt.6, f32[]{:T(128)S(6)} %mul.86), kind=kOutput, calls=%fused_computation.8 | convolution fusion | flops 7520780288 | bytes 22544392 | tf_op jit(solution)/shard_map/dot_general | solution.py:16
  449.1 0.0 all-gather.13.cloned.1.call-update
  449.1 0.2 reduce-scatter.5.cloned.1.call-start
  449.3 80.8 %all-gather.13.cloned.1.call-done = bf16[4096,1792]{1,0:T(8,128)(2,1)} async-done(((bf16[512,1792]{1,0:T(8,128)(2,1)}), bf16[4096,1792]{1,0:T(8,128)(2,1)}) %all-gather.13.cloned.1.call-update) | async-done | bytes 14680080 | tf_op jit(solution)/shard_map/all_gather | solution.py:25
  530.1 13.5 %fusion.10 = f32[512,4096]{1,0:T(8,128)} fusion(bf16[512,1792]{1,0:T(8,128)(2,1)} %fusion.2, bf16[4096,1792]{1,0:T(8,128)(2,1)} %all-gather.13.cloned.1.call-done), kind=kOutput, calls=%fused_computation.18 | convolution fusion | flops 7516192768 | bytes 24903680 | tf_op jit(solution)/shard_map/dot_general | solution.py:27
  543.7 0.0 reduce-scatter.5.cloned.1.call-update
  543.7 0.0 copy-start.1
  543.7 0.0 all-gather.15.cloned.1.call-start
  543.7 144.7 %reduce-scatter.5.cloned.1.call-done = f32[128,4096]{1,0:T(8,128)} async-done(((f32[512,4096]{1,0:T(8,128)}), f32[128,4096]{1,0:T(8,128)}) %reduce-scatter.5.cloned.1.call-update) | async-done | bytes 2097168 | tf_op jit(solution)/shard_map/reduce_scatter | solution.py:26
  688.5 3.7 multiply_reduce_fusion
  692.1 0.0 all-gather.15.cloned.1.call-update
  692.1 0.0 all-gather.17.cloned.1.call-start
  692.2 46.6 %psum.15 = f32[]{:T(128)} all-reduce(f32[]{:T(128)} %get-tuple-element.2), channel_id=1, replica_groups=mesh['dp'=8,'shard'=4] {'dp','shard'}, use_global_device_ids=true, to_apply=%region_5.0 | all-reduce | flops 1 | bytes 8 | tf_op jit(solution)/shard_map/psum | solution.py:36
  739.5 35.1 %all-gather.15.cloned.1.call-done = bf16[512,4096]{1,0:T(8,128)(2,1)} async-done(((bf16[128,4096]{1,0:T(8,128)(2,1)}), bf16[512,4096]{1,0:T(8,128)(2,1)}) %all-gather.15.cloned.1.call-update) | async-done | bytes 4194320 | tf_op jit(solution)/shard_map/all_gather | solution.py:35
  774.6 0.0 copy-done.1
  774.6 14.2 %fusion.8 = bf16[512,1792]{1,0:T(8,128)(2,1)} fusion(bf16[512,1792]{1,0:T(8,128)(2,1)S(1)} %copy-done.1, bf16[512,4096]{1,0:T(8,128)(2,1)} %all-gather.15.cloned.1.call-done, bf16[4096,1792]{1,0:T(8,128)(2,1)} %all-gather.13.cloned.1.call-done, f32[]{:T(128)S(6)} %mul.106, f32[]{:T(128)S(6)} %mul.102), kind=kOutput, calls=%fused_computation.14 | convolution fusion | flops 7520780288 | bytes 22544392 | tf_op jit(solution)/shard_map/dot_general | solution.py:16
  788.8 0.0 all-gather.17.cloned.1.call-update
  788.8 79.5 %all-gather.17.cloned.1.call-done = bf16[4096,1792]{1,0:T(8,128)(2,1)} async-done(((bf16[512,1792]{1,0:T(8,128)(2,1)}), bf16[4096,1792]{1,0:T(8,128)(2,1)}) %all-gather.17.cloned.1.call-update) | async-done | bytes 14680080 | tf_op jit(solution)/shard_map/all_gather | solution.py:45
  868.3 14.5 %fusion.6 = f32[512,1792]{1,0:T(8,128)} fusion(bf16[512,1792]{1,0:T(8,128)(2,1)S(1)} %copy-done.1, bf16[512,4096]{1,0:T(8,128)(2,1)} %all-gather.15.cloned.1.call-done, bf16[4096,1792]{1,0:T(8,128)(2,1)} %all-gather.17.cloned.1.call-done, f32[]{:T(128)S(6)} %rsqrt.7, f32[]{:T(128)S(6)} %mul.98), kind=kOutput, calls=%fused_computation.12 | convolution fusion | flops 7520780288 | bytes 24379400 | tf_op jit(solution)/shard_map/dot_general | solution.py:16
Async XLA Ops:
  7.2 89.5 %all-gather.7.cloned.1.call-start = ((), (), s32[]{:S(2)}) async-start(), calls=%async_computation.2 | async-start | bytes 16515072 | tf_op jit(solution)/shard_map/all_gather | solution.py:25
  12.9 242.1 %reduce-scatter.3.cloned.1.call-start = ((), (), s32[]{:S(2)}) async-start(), calls=%async_computation.3 | async-start | bytes 10485760 | tf_op jit(solution)/shard_map/reduce_scatter | solution.py:26
  110.2 230.9 %copy-start = (bf16[512,1792]{1,0:T(8,128)(2,1)S(1)}, bf16[512,1792]{1,0:T(8,128)(2,1)}, u32[]{:S(2)}) copy-start(bf16[512,1792]{1,0:T(8,128)(2,1)} %get-tuple-element.6) | copy-start | bytes 5505028
  110.2 230.9 %all-gather.9.cloned.1.call-start = ((), (), s32[]{:S(2)}) async-start(), calls=%async_computation.4 | async-start | bytes 5242880 | tf_op jit(solution)/shard_map/all_gather | solution.py:35
  258.7 176.2 %all-gather.11.cloned.1.call-start = ((), (), s32[]{:S(2)}) async-start(), calls=%async_computation.5 | async-start | bytes 16515072 | tf_op jit(solution)/shard_map/all_gather | solution.py:45
  355.4 174.7 %all-gather.13.cloned.1.call-start = ((), (), s32[]{:S(2)}) async-start(), calls=%async_computation.6 | async-start | bytes 16515072 | tf_op jit(solution)/shard_map/all_gather | solution.py:25
  449.1 239.3 %reduce-scatter.5.cloned.1.call-start = ((), (), s32[]{:S(2)}) async-start(), calls=%async_computation.7 | async-start | bytes 10485760 | tf_op jit(solution)/shard_map/reduce_scatter | solution.py:26
  543.7 230.9 %copy-start.1 = (bf16[512,1792]{1,0:T(8,128)(2,1)S(1)}, bf16[512,1792]{1,0:T(8,128)(2,1)}, u32[]{:S(2)}) copy-start(bf16[512,1792]{1,0:T(8,128)(2,1)} %fusion.2) | copy-start | bytes 5505028
  543.7 230.9 %all-gather.15.cloned.1.call-start = ((), (), s32[]{:S(2)}) async-start(), calls=%async_computation.8 | async-start | bytes 5242880 | tf_op jit(solution)/shard_map/all_gather | solution.py:35
  692.1 176.2 %all-gather.17.cloned.1.call-start = ((), (), s32[]{:S(2)}) async-start(), calls=%async_computation.9 | async-start | bytes 16515072 | tf_op jit(solution)/shard_map/all_gather | solution.py:45
Sparse Core Ops, SparseCore 0:
  13.0 83.5 all-gather.6
  110.3 144.6 reduce-scatter.2
  258.8 82.2 all-gather.8
  355.5 79.3 all-gather.10
  449.2 80.8 all-gather.12
  543.8 144.6 reduce-scatter.4
  692.3 82.2 all-gather.14
  789.0 79.3 all-gather.16
where the time goes:
time: 890 us
  waiting for transfers between devices  683 us (77%)
  blocking collectives  93.2 us (10%)
  matrix products  84.2 us (9%)
  between operations  15.6 us (2%)
  other arithmetic  13 us (1%)
    reduce_scatter x2, waiting for transfers between devices, body(): lax.psum_scatter(lax.dot_general(matrix, column_panel, (((1,), (1,)), (()...  289 us
    all_gather x2, waiting for transfers between devices, body(): column_panel = lax.all_gather(matrix, 'dp', axis=0, tiled=True)  164 us
    all_gather x2, waiting for transfers between devices, body(): lax.all_gather(mixture, 'dp', axis=0, tiled=True)  159 us
    psum x2, blocking collectives, body(): lax.psum(jnp.sum(jnp.square(gram_part.astype(jnp.float32))), ('dp', 'shar...  93.2 us
    all_gather x2, waiting for transfers between devices, body(): gram_panel = lax.all_gather(gram_part, 'shard', axis=0, tiled=True)  70.1 us
    dot_general x4, matrix products, apply_panel(): return jnp.dot(gram_panel, right_side, preferred_element_type=jnp.float32)  57.1 us
    dot_general x2, matrix products, body(): lax.dot_general(matrix, column_panel, (((1,), (1,)), ((), ())), preferred...  27.1 us
  transfers between devices with their start and end apart: 8, of which 8 were waited for; matrix products, arithmetic and copies ran while one was open for 0% of the time, Pallas kernels for 0%

commit v1 on v0

--- a/solution.py
+++ b/solution.py
@@ -10,6 +10,27 @@
 linear_term = 3.4445
 cubic_term = -4.775
 quintic_term = 2.0315
+
+
+def collect(value, axis, dim):
+    size, here, rows = (lax.axis_size(axis), lax.axis_index(axis), value.shape[dim])
+    ahead = [(i, (i + 1) % size) for i in range(size)]
+    left = [(i, (i - 1) % size) for i in range(size)]
+    whole = jnp.zeros((*value.shape[:dim], size * rows, *value.shape[dim + 1 :]), value.dtype)
+    whole = lax.dynamic_update_slice_in_dim(whole, value, here * rows, axis=dim)
+    from_left = from_right = value
+    halfway = size // 2
+    for lap in range(1, halfway + 1):
+        from_left = lax.ppermute(from_left, axis, ahead)
+        whole = lax.dynamic_update_slice_in_dim(
+            whole, from_left, (here - lap) % size * rows, axis=dim
+        )
+        if lap < size - halfway:
+            from_right = lax.ppermute(from_right, axis, left)
+            whole = lax.dynamic_update_slice_in_dim(
+                whole, from_right, (here + lap) % size * rows, axis=dim
+            )
+    return whole
 
 
 def apply_panel(gram_panel, right_side):
@@ -32,7 +53,7 @@
             tiled=True,
         )
         gram_part = summed_part.astype(jnp.bfloat16)
-        gram_panel = lax.all_gather(gram_part, "shard", axis=0, tiled=True)
+        gram_panel = collect(gram_part, "shard", 0)
         square_sum = lax.psum(jnp.sum(jnp.square(gram_part.astype(jnp.float32))), ("dp", "shard"))
         inverse_norm = lax.rsqrt(square_sum)
         root_scale = jnp.sqrt(inverse_norm)

time: 890 us -> 927 us (1.042)
  starting transfers between devices: 0.51 us -> 50.6 us
  waiting for transfers between devices: 683 us -> 663 us
  local copies, waits for them, and re-layouts: 0.01 us -> 18.9 us
  blocking collectives: 93.2 us -> 82.9 us
    all_gather x2 -> x0, waiting for transfers between devices: 70.1 us -> none  [body(): gram_panel = lax.all_gather(gram_part, 'shard', axis=0, tiled=True)]
    ppermute x0 -> x6, starting transfers between devices: none -> 50.1 us  [the longest x4 44.6 us: collect(): from_left = lax.ppermute(from_left, axis, ahead)]
    ppermute x0 -> x6, waiting for transfers between devices: none -> 48.3 us  [the longest x4 48.3 us: collect(): from_left = lax.ppermute(from_left, axis, ahead)]
    dynamic_update_slice x0 -> x8, local copies, waits for them, and re-layouts: none -> 14 us  [the longest x4 9.23 us: collect(): lax.dynamic_update_slice_in_dim(whole, from_left, (here - lap) % size * r...]
    psum x2, blocking collectives: 93.2 us -> 82.9 us  [body(): lax.psum(jnp.sum(jnp.square(gram_part.astype(jnp.float32))), ('dp', 'shar...]
  transfers between devices with their start and end apart: 8 -> 12, of which waited for: 8 -> 8; matrix products, arithmetic and copies ran while one was open for 0% -> 1% of each run, Pallas kernels for 0% -> 0%
where the time goes in v1:
time: 927 us; the launch traced here: 926 us
  waiting for transfers between devices  663 us (72%)
  matrix products  84.3 us (9%)
  blocking collectives  82.9 us (9%)
  starting transfers between devices  50.6 us (5%)
  local copies, waits for them, and re-layouts  18.9 us (2%)
  between operations  15.6 us (2%)
  other arithmetic  11.2 us (1%)
    reduce_scatter x2, waiting for transfers between devices, body(): lax.psum_scatter(lax.dot_general(matrix, column_panel, (((1,), (1,)), (()...  289 us
    all_gather x2, waiting for transfers between devices, body(): column_panel = lax.all_gather(matrix, 'dp', axis=0, tiled=True)  164 us
    all_gather x2, waiting for transfers between devices, body(): lax.all_gather(mixture, 'dp', axis=0, tiled=True)  161 us
    psum x2, blocking collectives, body(): lax.psum(jnp.sum(jnp.square(gram_part.astype(jnp.float32))), ('dp', 'shar...  82.9 us
    dot_general x4, matrix products, apply_panel(): return jnp.dot(gram_panel, right_side, preferred_element_type=jnp.float32)  57.2 us
    ppermute x4, waiting for transfers between devices, collect(): from_left = lax.ppermute(from_left, axis, ahead)  48.3 us
    ppermute x4, starting transfers between devices, collect(): from_left = lax.ppermute(from_left, axis, ahead)  44.6 us
    dot_general x2, matrix products, body(): lax.dot_general(matrix, column_panel, (((1,), (1,)), ((), ())), preferred...  27.1 us
  transfers between devices with their start and end apart: 12, of which 8 were waited for; matrix products, arithmetic and copies ran while one was open for 1% of the time, Pallas kernels for 0%

profile of v1, /device:TPU:0, one launch (start us, length us, event | category | flops | bytes accessed | tf_op | source)
XLA Modules:
  0.0 926.5 jit_solution(4461363610900703909)
XLA Ops:
  7.2 0.0 all-gather.5.cloned.1.call-start
  7.2 5.7 fusion
  12.9 0.0 all-gather.5.cloned.1.call-update
  12.9 0.0 reduce-scatter.3.cloned.1.call-start
  13.0 83.7 %all-gather.5.cloned.1.call-done = bf16[4096,1792]{1,0:T(8,128)(2,1)} async-done(((bf16[512,1792]{1,0:T(8,128)(2,1)}), bf16[4096,1792]{1,0:T(8,128)(2,1)}) %all-gather.5.cloned.1.call-update) | async-done | bytes 14680080 | tf_op jit(solution)/shard_map/all_gather | solution.py:46
  96.7 13.5 %fusion.9 = f32[512,4096]{1,0:T(8,128)} fusion(bf16[512,1792]{1,0:T(8,128)(2,1)} %get-tuple-element.6, bf16[4096,1792]{1,0:T(8,128)(2,1)} %all-gather.5.cloned.1.call-done), kind=kOutput, calls=%fused_computation.25 | convolution fusion | flops 7516192768 | bytes 24903680 | tf_op jit(solution)/shard_map/dot_general | solution.py:48
  110.2 0.0 reduce-scatter.3.cloned.1.call-update
  110.2 0.0 all-gather.7.cloned.1.call-start
  110.3 144.7 %reduce-scatter.3.cloned.1.call-done = f32[128,4096]{1,0:T(8,128)} async-done(((f32[512,4096]{1,0:T(8,128)}), f32[128,4096]{1,0:T(8,128)}) %reduce-scatter.3.cloned.1.call-update) | async-done | bytes 2097168 | tf_op jit(solution)/shard_map/reduce_scatter | solution.py:47
  255.0 2.8 multiply_reduce_fusion.1
  257.8 1.1 collective-permute-start
  258.8 2.8 collective-permute-start.1
  261.6 24.2 %collective-permute-done = bf16[128,4096]{1,0:T(8,128)(2,1)} collective-permute-done((bf16[128,4096]{1,0:T(8,128)(2,1)S(1)}, bf16[128,4096]{1,0:T(8,128)(2,1)}, u32[]{:S(2)}, u32[]{:S(2)}) %collective-permute-start) | collective-permute-done | bytes 1048608 | tf_op jit(solution)/shard_map/ppermute | solution.py:24
  285.7 21.3 %collective-permute-start.2 = (bf16[128,4096]{1,0:T(8,128)(2,1)}, bf16[128,4096]{1,0:T(8,128)(2,1)}, u32[]{:S(2)}, u32[]{:S(2)}) collective-permute-start(bf16[128,4096]{1,0:T(8,128)(2,1)} %collective-permute-done), channel_id=1, source_target_pairs={{0,1},{1,2},{2,3},{3,0},{4,5},{5,6},{6,7},{7,4},{8,9},{9,10},{10,1... | collective-permute-start | bytes 3145736 | tf_op jit(solution)/shard_map/ppermute | solution.py:24
  307.0 0.5 broadcast.10.clone
  307.5 0.1 constant_dynamic-update-slice_fusion.7
  307.6 0.0 copy-start.2
  307.6 1.9 copy-done.2
  309.6 0.0 copy-start
  309.6 41.5 %psum.14 = f32[]{:T(128)} all-reduce(f32[]{:T(128)} %get-tuple-element.4), channel_id=1, replica_groups=mesh['dp'=8,'shard'=4] {'dp','shard'}, use_global_device_ids=true, to_apply=%region_2.3 | all-reduce | flops 1 | bytes 8 | tf_op jit(solution)/shard_map/psum | solution.py:57
  351.7 2.3 constant_dynamic-update-slice_fusion.6
  354.1 0.0 collective-permute-done.1
  354.1 2.3 constant_dynamic-update-slice_fusion.5
  356.4 0.0 collective-permute-done.2
  356.4 2.3 constant_dynamic-update-slice_fusion.4
  358.6 0.0 copy-done
  358.6 14.2 %fusion.4 = bf16[512,1792]{1,0:T(8,128)(2,1)} fusion(bf16[512,1792]{1,0:T(8,128)(2,1)S(1)} %copy-done, bf16[512,4096]{1,0:T(8,128)(2,1)} %constant_dynamic-update-slice_fusion.4, bf16[4096,1792]{1,0:T(8,128)(2,1)} %all-gather.5.cloned.1.call-done, f32[]{:T(128)S(6)} %mul.114, f32[]{:T(128)S(6)} %mul.110), kind=kOutput, calls=%fused_computation.10 | convolution fusion | flops 7520780288 | bytes 22544392 | tf_op jit(solution)/shard_map/dot_general | solution.py:37
  372.9 0.0 all-gather.7.cloned.1.call-update
  372.9 0.0 all-gather.9.cloned.1.call-start
  373.0 80.3 %all-gather.7.cloned.1.call-done = bf16[4096,1792]{1,0:T(8,128)(2,1)} async-done(((bf16[512,1792]{1,0:T(8,128)(2,1)}), bf16[4096,1792]{1,0:T(8,128)(2,1)}) %all-gather.7.cloned.1.call-update) | async-done | bytes 14680080 | tf_op jit(solution)/shard_map/all_gather | solution.py:66
  453.2 14.2 %fusion.2 = bf16[512,1792]{1,0:T(8,128)(2,1)} fusion(bf16[512,1792]{1,0:T(8,128)(2,1)S(1)} %copy-done, bf16[512,4096]{1,0:T(8,128)(2,1)} %constant_dynamic-update-slice_fusion.4, bf16[4096,1792]{1,0:T(8,128)(2,1)} %all-gather.7.cloned.1.call-done, f32[]{:T(128)S(6)} %rsqrt.6, f32[]{:T(128)S(6)} %mul.102), kind=kOutput, calls=%fused_computation.8 | convolution fusion | flops 7520780288 | bytes 22544392 | tf_op jit(solution)/shard_map/dot_general | solution.py:37
  467.5 0.0 all-gather.9.cloned.1.call-update
  467.5 0.2 reduce-scatter.5.cloned.1.call-start
  467.7 80.8 %all-gather.9.cloned.1.call-done = bf16[4096,1792]{1,0:T(8,128)(2,1)} async-done(((bf16[512,1792]{1,0:T(8,128)(2,1)}), bf16[4096,1792]{1,0:T(8,128)(2,1)}) %all-gather.9.cloned.1.call-update) | async-done | bytes 14680080 | tf_op jit(solution)/shard_map/all_gather | solution.py:46
  548.5 13.5 %fusion.10 = f32[512,4096]{1,0:T(8,128)} fusion(bf16[512,1792]{1,0:T(8,128)(2,1)} %fusion.2, bf16[4096,1792]{1,0:T(8,128)(2,1)} %all-gather.9.cloned.1.call-done), kind=kOutput, calls=%fused_computation.26 | convolution fusion | flops 7516192768 | bytes 24903680 | tf_op jit(solution)/shard_map/dot_general | solution.py:48
  562.0 0.0 reduce-scatter.5.cloned.1.call-update
  562.1 0.0 all-gather.11.cloned.1.call-start
  562.1 144.7 %reduce-scatter.5.cloned.1.call-done = f32[128,4096]{1,0:T(8,128)} async-done(((f32[512,4096]{1,0:T(8,128)}), f32[128,4096]{1,0:T(8,128)}) %reduce-scatter.5.cloned.1.call-update) | async-done | bytes 2097168 | tf_op jit(solution)/shard_map/reduce_scatter | solution.py:47
  706.8 2.8 multiply_reduce_fusion
  709.6 1.1 collective-permute-start.3
  710.7 2.8 collective-permute-start.4
  713.4 24.2 %collective-permute-done.3 = bf16[128,4096]{1,0:T(8,128)(2,1)} collective-permute-done((bf16[128,4096]{1,0:T(8,128)(2,1)S(1)}, bf16[128,4096]{1,0:T(8,128)(2,1)}, u32[]{:S(2)}, u32[]{:S(2)}) %collective-permute-start.3) | collective-permute-done | bytes 1048608 | tf_op jit(solution)/shard_map/ppermute | solution.py:24
  737.6 21.2 %collective-permute-start.5 = (bf16[128,4096]{1,0:T(8,128)(2,1)}, bf16[128,4096]{1,0:T(8,128)(2,1)}, u32[]{:S(2)}, u32[]{:S(2)}) collective-permute-start(bf16[128,4096]{1,0:T(8,128)(2,1)} %collective-permute-done.3), channel_id=1, source_target_pairs={{0,1},{1,2},{2,3},{3,0},{4,5},{5,6},{6,7},{7,4},{8,9},{9,10},{10,1... | collective-permute-start | bytes 3145736 | tf_op jit(solution)/shard_map/ppermute | solution.py:24
  758.8 0.5 broadcast.10
  759.3 0.1 constant_dynamic-update-slice_fusion.3
  759.4 0.0 copy-start.1
  759.4 1.9 copy-done.1
  761.4 0.0 copy-start.3
  761.4 41.5 %psum.15 = f32[]{:T(128)} all-reduce(f32[]{:T(128)} %get-tuple-element.2), channel_id=1, replica_groups=mesh['dp'=8,'shard'=4] {'dp','shard'}, use_global_device_ids=true, to_apply=%region_5.6 | all-reduce | flops 1 | bytes 8 | tf_op jit(solution)/shard_map/psum | solution.py:57
  803.6 2.3 constant_dynamic-update-slice_fusion.2
  805.9 0.0 collective-permute-done.4
  805.9 2.3 constant_dynamic-update-slice_fusion.1
  808.2 0.0 collective-permute-done.5
  808.2 2.3 constant_dynamic-update-slice_fusion
  810.5 0.0 copy-done.3
  810.5 14.2 %fusion.8 = bf16[512,1792]{1,0:T(8,128)(2,1)} fusion(bf16[512,1792]{1,0:T(8,128)(2,1)S(1)} %copy-done.3, bf16[512,4096]{1,0:T(8,128)(2,1)} %constant_dynamic-update-slice_fusion, bf16[4096,1792]{1,0:T(8,128)(2,1)} %all-gather.9.cloned.1.call-done, f32[]{:T(128)S(6)} %mul.126, f32[]{:T(128)S(6)} %mul.122), kind=kOutput, calls=%fused_computation.14 | convolution fusion | flops 7520780288 | bytes 22544392 | tf_op jit(solution)/shard_map/dot_general | solution.py:37
  824.7 0.0 all-gather.11.cloned.1.call-update
  824.7 80.3 %all-gather.11.cloned.1.call-done = bf16[4096,1792]{1,0:T(8,128)(2,1)} async-done(((bf16[512,1792]{1,0:T(8,128)(2,1)}), bf16[4096,1792]{1,0:T(8,128)(2,1)}) %all-gather.11.cloned.1.call-update) | async-done | bytes 14680080 | tf_op jit(solution)/shard_map/all_gather | solution.py:66
  905.1 14.5 %fusion.6 = f32[512,1792]{1,0:T(8,128)} fusion(bf16[512,1792]{1,0:T(8,128)(2,1)S(1)} %copy-done.3, bf16[512,4096]{1,0:T(8,128)(2,1)} %constant_dynamic-update-slice_fusion, bf16[4096,1792]{1,0:T(8,128)(2,1)} %all-gather.11.cloned.1.call-done, f32[]{:T(128)S(6)} %rsqrt.7, f32[]{:T(128)S(6)} %mul.118), kind=kOutput, calls=%fused_computation.12 | convolution fusion | flops 7520780288 | bytes 24379400 | tf_op jit(solution)/shard_map/dot_general | solution.py:37
Async XLA Ops:
  7.2 89.5 %all-gather.5.cloned.1.call-start = ((), (), s32[]{:S(2)}) async-start(), calls=%async_computation.2 | async-start | bytes 16515072 | tf_op jit(solution)/shard_map/all_gather | solution.py:46
  12.9 242.1 %reduce-scatter.3.cloned.1.call-start = ((), (), s32[]{:S(2)}) async-start(), calls=%async_computation.3 | async-start | bytes 10485760 | tf_op jit(solution)/shard_map/reduce_scatter | solution.py:47
  110.2 343.0 %all-gather.7.cloned.1.call-start = ((), (), s32[]{:S(2)}) async-start(), calls=%async_computation.4 | async-start | bytes 16515072 | tf_op jit(solution)/shard_map/all_gather | solution.py:66
  257.8 28.0 %collective-permute-start = (bf16[128,4096]{1,0:T(8,128)(2,1)S(1)}, bf16[128,4096]{1,0:T(8,128)(2,1)}, u32[]{:S(2)}, u32[]{:S(2)}) collective-permute-start(bf16[128,4096]{1,0:T(8,128)(2,1)S(1)} %get-tuple-element.5), channel_id=1, source_target_pairs={{0,1},{1,2},{2,3},{3,0},{4,5},{5,6},{6,7},{7,4},{8,9},{9,10},{10,1... | collective-permute-start | bytes 3145736 | tf_op jit(solution)/shard_map/ppermute | solution.py:24
  258.8 95.2 %collective-permute-start.1 = (bf16[128,4096]{1,0:T(8,128)(2,1)S(1)}, bf16[128,4096]{1,0:T(8,128)(2,1)}, u32[]{:S(2)}, u32[]{:S(2)}) collective-permute-start(bf16[128,4096]{1,0:T(8,128)(2,1)S(1)} %get-tuple-element.5), channel_id=1, source_target_pairs={{0,3},{1,0},{2,1},{3,2},{4,7},{5,4},{6,5},{7,6},{8,11},{9,8},{10,9... | collective-permute-start | bytes 3145736 | tf_op jit(solution)/shard_map/ppermute | solution.py:29
  285.7 70.6 %collective-permute-start.2 = (bf16[128,4096]{1,0:T(8,128)(2,1)}, bf16[128,4096]{1,0:T(8,128)(2,1)}, u32[]{:S(2)}, u32[]{:S(2)}) collective-permute-start(bf16[128,4096]{1,0:T(8,128)(2,1)} %collective-permute-done), channel_id=1, source_target_pairs={{0,1},{1,2},{2,3},{3,0},{4,5},{5,6},{6,7},{7,4},{8,9},{9,10},{10,1... | collective-permute-start | bytes 3145736 | tf_op jit(solution)/shard_map/ppermute | solution.py:24
  307.6 2.0 copy-start.2
  309.6 49.1 %copy-start = (bf16[512,1792]{1,0:T(8,128)(2,1)S(1)}, bf16[512,1792]{1,0:T(8,128)(2,1)}, u32[]{:S(2)}) copy-start(bf16[512,1792]{1,0:T(8,128)(2,1)} %get-tuple-element.6) | copy-start | bytes 5505028
  372.9 175.6 %all-gather.9.cloned.1.call-start = ((), (), s32[]{:S(2)}) async-start(), calls=%async_computation.5 | async-start | bytes 16515072 | tf_op jit(solution)/shard_map/all_gather | solution.py:46
  467.5 239.3 %reduce-scatter.5.cloned.1.call-start = ((), (), s32[]{:S(2)}) async-start(), calls=%async_computation.6 | async-start | bytes 10485760 | tf_op jit(solution)/shard_map/reduce_scatter | solution.py:47
  562.1 343.0 %all-gather.11.cloned.1.call-start = ((), (), s32[]{:S(2)}) async-start(), calls=%async_computation.7 | async-start | bytes 16515072 | tf_op jit(solution)/shard_map/all_gather | solution.py:66
  709.6 28.0 %collective-permute-start.3 = (bf16[128,4096]{1,0:T(8,128)(2,1)S(1)}, bf16[128,4096]{1,0:T(8,128)(2,1)}, u32[]{:S(2)}, u32[]{:S(2)}) collective-permute-start(bf16[128,4096]{1,0:T(8,128)(2,1)S(1)} %get-tuple-element.3), channel_id=1, source_target_pairs={{0,1},{1,2},{2,3},{3,0},{4,5},{5,6},{6,7},{7,4},{8,9},{9,10},{10,1... | collective-permute-start | bytes 3145736 | tf_op jit(solution)/shard_map/ppermute | solution.py:24
  710.7 95.2 %collective-permute-start.4 = (bf16[128,4096]{1,0:T(8,128)(2,1)S(1)}, bf16[128,4096]{1,0:T(8,128)(2,1)}, u32[]{:S(2)}, u32[]{:S(2)}) collective-permute-start(bf16[128,4096]{1,0:T(8,128)(2,1)S(1)} %get-tuple-element.3), channel_id=1, source_target_pairs={{0,3},{1,0},{2,1},{3,2},{4,7},{5,4},{6,5},{7,6},{8,11},{9,8},{10,9... | collective-permute-start | bytes 3145736 | tf_op jit(solution)/shard_map/ppermute | solution.py:29
  737.6 70.6 %collective-permute-start.5 = (bf16[128,4096]{1,0:T(8,128)(2,1)}, bf16[128,4096]{1,0:T(8,128)(2,1)}, u32[]{:S(2)}, u32[]{:S(2)}) collective-permute-start(bf16[128,4096]{1,0:T(8,128)(2,1)} %collective-permute-done.3), channel_id=1, source_target_pairs={{0,1},{1,2},{2,3},{3,0},{4,5},{5,6},{6,7},{7,4},{8,9},{9,10},{10,1... | collective-permute-start | bytes 3145736 | tf_op jit(solution)/shard_map/ppermute | solution.py:24
  759.4 2.0 copy-start.1
  761.4 49.1 %copy-start.3 = (bf16[512,1792]{1,0:T(8,128)(2,1)S(1)}, bf16[512,1792]{1,0:T(8,128)(2,1)}, u32[]{:S(2)}) copy-start(bf16[512,1792]{1,0:T(8,128)(2,1)} %fusion.2) | copy-start | bytes 5505028
Sparse Core Ops, SparseCore 0:
  13.0 83.5 all-gather.4
  110.3 144.6 reduce-scatter.2
  373.0 80.1 all-gather.6
  467.6 80.8 all-gather.8
  562.2 144.6 reduce-scatter.4
  824.9 80.1 all-gather.10
